TPU v7x, 32 devices: a whole 2x2x4 slice. The times are simulated.
32 devices in a mesh: seq: 8 (over z, x), head: 4 (over y, core).
Axes of the slice: x: 2, y: 2, z: 4, core: 2. Of those that a mesh axis runs over, the one named last changes fastest.
Arguments:
- x_in: bfloat16 [2048, 4096], P('seq', 'head'), may hold values from -6 to 6
- z_gate: bfloat16 [2048, 4096], P('seq', 'head'), may hold values from -8 to 8
- b_proj: bfloat16 [2048, 4, 256], P('seq', 'head'), may hold values from -6 to 6
- c_proj: bfloat16 [2048, 4, 256], P('seq', 'head'), may hold values from -6 to 6
- log_decay: float32 [2048, 64], P('seq', 'head'), may hold values from -1 to 0
- norm_gain: float32 [4096], P('head'), may hold values from 0.5 to 1.5
- w_out: bfloat16 [4096, 8192], P('head', 'seq'), may hold values from -0.125 to 0.125
Outputs:
- mixed: bfloat16 [2048, 8192], P('seq', 'head')
All inputs are finite; a program needn't handle non-finite values.
Results may differ from a plain program's by a relative error of at most 0.015.
Values may be sent and summed in bfloat16 or wider, within the bound.
No kernel may reach another device: no remote copies, remote signals or barrier semaphores. Data moves between devices by JAX's collectives and lax.ppermute only.
A program may use at most 128 MiB of HBM per device.

v0:
```python
import jax
import jax.numpy as jnp
from jax import lax
from jax.sharding import PartitionSpec as P


def carried_in(value, axis, combine, identity):
    count, place = (lax.axis_size(axis), lax.axis_index(axis))
    everything = jax.tree.map(
        lambda part, kind: lax.all_gather(part.astype(kind), axis),
        value,
        (jnp.bfloat16, jnp.bfloat16),
    )
    start = jax.tree.map(
        lambda part, zero: jnp.broadcast_to(jnp.asarray(zero, part.dtype), part.shape),
        value,
        identity,
    )

    def hop(k, before):
        reached = k < place
        new = combine(
            before, jax.tree.map(lambda part, own: part[k].astype(own.dtype), everything, value)
        )
        return jax.tree.map(lambda a, b: jnp.where(reached, a, b), new, before)

    return lax.fori_loop(0, count, hop, start)


def combine(earlier, later):
    return (earlier[0] * later[0], later[0][:, None, None] * earlier[1] + later[1])


def carry_in(decay_total, state):
    identity = (jnp.ones_like(decay_total), jnp.zeros_like(state))
    return carried_in((decay_total, state), "seq", combine, identity)


def body(x_in, z_gate, b_proj, c_proj, log_decay, norm_gain, w_out):
    rows = x_in.shape[0]
    heads = log_decay.shape[1]
    head_dim = x_in.shape[1] // heads
    b_local = b_proj[:, 0, :]
    c_local = c_proj[:, 0, :]
    x_heads = x_in.reshape(rows, heads, head_dim)
    cum = jnp.cumsum(log_decay, axis=0)
    total = cum[-1]
    scores = jnp.dot(c_local, b_local.T, preferred_element_type=jnp.float32)
    index = jnp.arange(rows)
    causal = (index[:, None] >= index[None, :])[None]
    cum_t = cum.T
    diff = cum_t[:, :, None] - cum_t[:, None, :]
    mask = jnp.where(causal, jnp.exp(jnp.where(causal, diff, 0.0)), 0.0)
    weighted = (mask * scores[None]).astype(jnp.bfloat16)
    y_intra = jnp.einsum("hij,jhp->ihp", weighted, x_heads, preferred_element_type=jnp.float32)
    weights = jnp.exp(total[None, :] - cum)
    scaled = (weights[:, :, None] * x_heads.astype(jnp.float32)).astype(jnp.bfloat16)
    state = jnp.einsum("thp,tn->hpn", scaled, b_local, preferred_element_type=jnp.float32)
    carried = carry_in(jnp.exp(total), state)
    state_in = carried[1].astype(jnp.bfloat16)
    y_state = jnp.exp(cum)[:, :, None] * jnp.einsum(
        "tn,hpn->thp", c_local, state_in, preferred_element_type=jnp.float32
    )
    y_all = (y_intra + y_state).reshape(rows, heads * head_dim)
    gated = y_all * jax.nn.silu(z_gate.astype(jnp.float32))
    mean_sq = jnp.mean(gated * gated, axis=1, keepdims=True)
    hidden = (gated * lax.rsqrt(mean_sq + 1e-05) * norm_gain[None, :]).astype(jnp.bfloat16)
    partial_terms = jnp.dot(
        hidden, lax.all_gather(w_out, "seq", axis=1, tiled=True), preferred_element_type=jnp.float32
    )
    mixed = lax.psum_scatter(
        partial_terms.astype(jnp.bfloat16), "head", scatter_dimension=1, tiled=True
    )
    return mixed


def solution(mesh):
    placed = (
        P("seq", "head"),
        P("seq", "head"),
        P("seq", "head", None),
        P("seq", "head", None),
        P("seq", "head"),
        P("head"),
        P("head", "seq"),
    )
    return jax.shard_map(
        body, mesh=mesh, in_specs=placed, out_specs=P("seq", "head"), check_vma=False
    )
```

profile of v0, /device:TPU:0, one launch (start us, length us, event | category | flops | bytes accessed | tf_op | source)
XLA Modules:
  0.0 377.3 jit_solution(7258897654931674551)
XLA Ops:
  6.5 0.0 copy-start
  6.5 0.0 copy-start.1
  6.5 0.0 all-gather.7.cloned.1.call-start
  6.5 0.8 copy_bitcast_fusion.1
  7.3 0.6 reduce-window.6
  7.9 0.2 slice_reduce_fusion
  8.1 0.1 fusion.25
  8.2 0.2 slice_reduce_fusion.1
  8.3 0.1 bitcast_exponential_fusion
  8.4 1.2 copy.27
  9.7 0.1 fusion.14
  9.8 0.0 copy-done
  9.8 1.1 convolution_convert_fusion.1
  10.9 0.0 all-gather.7.cloned.1.call-update
  10.9 0.0 all-gather.5.cloned.1.call-start
  11.0 0.7 all-gather.5.cloned.1.call-update
  11.7 0.0 reduce-scatter.2.cloned.1.call-start
  11.7 0.2 fusion.23
  11.9 22.2 %all-gather.1 = bf16[8,1,16]{2,1,0:T(2,128)(2,1)S(1)} all-gather(bf16[1,1,16]{2,1,0:T(2,128)(2,1)S(1)} %bitcast.72), channel_id=1, replica_groups=mesh['seq'=8,'head'=4] {'seq'}, dimensions={0}, use_global_device_ids=true | all-gather | bytes 288 | tf_op jit(solution)/shard_map/all_gather | solution.py:10
  34.2 0.0 copy-done.1
  34.2 0.2 fusion.20
  34.4 1.2 fusion.7
  35.6 51.5 %all-gather.7.cloned.1.call-done = bf16[128,64,256]{2,1,0:T(8,128)(2,1)} async-done(((bf16[16,64,256]{2,1,0:T(8,128)(2,1)}), bf16[128,64,256]{2,1,0:T(8,128)(2,1)}) %all-gather.7.cloned.1.call-update) | async-done | bytes 4194320 | tf_op jit(solution)/shard_map/all_gather | solution.py:10
  87.2 10.9 %while.14 = (s32[]{:T(128)}, f32[16,64,256]{2,1,0:T(8,128)S(1)}, s32[]{:T(128)}, bf16[8,16]{1,0:T(8,128)(2,1)S(1)}, bf16[8,16,64,256]{3,2,1,0:T(8,128)(2,1)}, /*index=5*/s32[]{:T(128)}, s32[]{:T(128)}) while((s32[]{:T(128)}, f32[16,64,256]{2,1,0:T(8,128)S(1)}, s32[]{:T(128)}, bf16[8,16]{1,0:T(8,128)(2,1)S(1)}, ...), condition=%wide.region_3.4_spmd.clone, body=%wide.region_2.3_spmd.clone.sunk | while | flops 1310740 | bytes 2621705 | solution.py:27
  87.2 1.3 fusion.32
  88.5 1.3 fusion.32
  89.8 1.3 fusion.32
  91.2 1.3 fusion.32
  92.5 1.3 fusion.32
  93.8 1.4 fusion.32
  95.3 1.4 fusion.32
  96.7 1.3 fusion.32
  98.0 0.0 copy-start.2
  98.1 0.4 fusion.9
  98.4 0.3 copy.29
  98.8 1.6 multiply_reduce_fusion
  100.3 214.9 %all-gather.5.cloned.1.call-done = bf16[1024,8192]{1,0:T(8,128)(2,1)} async-done(((bf16[1024,1024]{1,0:T(8,128)(2,1)}), bf16[1024,8192]{1,0:T(8,128)(2,1)}) %all-gather.5.cloned.1.call-update) | async-done | bytes 16777232 | tf_op jit(solution)/shard_map/all_gather | solution.py:69
  315.3 0.0 copy-done.2
  315.3 12.6 %convolution_convert_fusion = bf16[256,8192]{1,0:T(8,128)(2,1)} fusion(bf16[1024,8192]{1,0:T(8,128)(2,1)} %all-gather.5.cloned.1.call-done, f32[1024]{0:T(1024)S(1)} %copy-done.2, f32[256]{0:T(256)S(1)} %add_rsqrt_fusion, f32[256,1024]{1,0:T(8,128)S(1)} %copy.29, bf16[256,1024]{1,0:T(8,128)(2,1)} %param.10), kind=kOutput, calls=%fused_computation.3 | convolution fusion | flops 4299423744 | bytes 22549504 | tf_op jit(solution)/shard_map/dot_general | solution.py:68
  327.9 0.0 reduce-scatter.2.cloned.1.call-update
  327.9 42.8 %reduce-scatter.2.cloned.1.call-done = bf16[256,2048]{1,0:T(8,128)(2,1)} async-done(((bf16[256,8192]{1,0:T(8,128)(2,1)}), bf16[256,2048]{1,0:T(8,128)(2,1)}) %reduce-scatter.2.cloned.1.call-update) | async-done | bytes 1048592 | tf_op jit(solution)/shard_map/reduce_scatter | solution.py:71
  (14 shorter events, 0.1 us)
Async XLA Ops:
  6.5 3.3 copy-start
  6.5 27.7 %copy-start.1 = (bf16[256,1,256]{2,0,1:T(8,128)(2,1)S(1)}, bf16[256,1,256]{2,0,1:T(8,128)(2,1)}, u32[]{:S(2)}) copy-start(bf16[256,1,256]{2,0,1:T(8,128)(2,1)} %param.12) | copy-start | bytes 393220
  6.5 80.6 %all-gather.7.cloned.1.call-start = ((), (), s32[]{:S(2)}) async-start(), calls=%async_computation.3 | async-start | bytes 4718592 | tf_op jit(solution)/shard_map/all_gather | solution.py:10
  10.9 304.3 %all-gather.5.cloned.1.call-start = ((), (), s32[]{:S(2)}) async-start(), calls=%async_computation.1 | async-start | bytes 18874368 | tf_op jit(solution)/shard_map/all_gather | solution.py:69
  11.7 359.1 %reduce-scatter.2.cloned.1.call-start = ((), (), s32[]{:S(2)}) async-start(), calls=%async_computation.2 | async-start | bytes 5242880 | tf_op jit(solution)/shard_map/reduce_scatter | solution.py:71
  98.0 217.2 %copy-start.2 = (f32[1024]{0:T(1024)S(1)}, f32[1024]{0:T(1024)}, u32[]{:S(2)}) copy-start(f32[1024]{0:T(1024)} %param.14) | copy-start | bytes 12292
Sparse Core Ops, SparseCore 0:
  11.0 76.0 all-gather.6
  89.4 225.8 all-gather.4
  328.0 42.6 reduce-scatter.1
where the time goes:
time: 378 us; the launch traced here: 377 us
  waiting for transfers between devices  310 us (82%)
  blocking collectives  22.2 us (6%)
  matrix products  15.5 us (4%)
  other arithmetic  13.3 us (4%)
  between operations  13.2 us (3%)
    all_gather x1, waiting for transfers between devices, body(): lax.all_gather(w_out, 'seq', axis=1, tiled=True)  215 us
    all_gather x1, waiting for transfers between devices, carried_in(): lax.all_gather(part.astype(kind), axis)  51.5 us
    reduce_scatter x1, waiting for transfers between devices, body(): lax.psum_scatter(partial_terms.astype(jnp.bfloat16), 'head', scatter_dime...  42.8 us
    all_gather x1, blocking collectives, carried_in(): lax.all_gather(part.astype(kind), axis)  22.2 us
    dot_general x1, matrix products, body(): jnp.dot(hidden, lax.all_gather(w_out, 'seq', axis=1, tiled=True), preferr...  12.6 us
    select_n x8, other arithmetic, hop(): return jax.tree.map(lambda a, b: jnp.where(reached, a, b), new, before)  10.6 us
  transfers between devices with their start and end apart: 3, of which 3 were waited for; matrix products, arithmetic and copies ran while one was open for 4% of the time, Pallas kernels for 0%

commit v1 on v0

--- a/solution.py
+++ b/solution.py
@@ -2,6 +2,23 @@
 import jax.numpy as jnp
 from jax import lax
 from jax.sharding import PartitionSpec as P
+from jax.lax import axis_index, axis_size, ppermute
+
+
+def mix_surface_by_axis(panel, along_axis):
+    devs = axis_size(along_axis)
+    pieces_in = [(idx, (idx + 1) % devs) for idx in range(devs)]
+    then, r2 = ([panel], [panel])
+    trail = [(idx, (idx - 1) % devs) for idx in range(devs)]
+    for _ in range(devs // 2):
+        then.append(ppermute(then[-1], along_axis, pieces_in))
+    for _ in [*range((devs - 1) // 2)]:
+        r2.append(ppermute(r2[-1], along_axis, trail))
+    return jnp.roll(
+        jnp.concatenate([*then[::-1], *r2[1:]], axis=1),
+        (axis_index(along_axis) - devs // 2) * panel.shape[1],
+        axis=1,
+    )
 
 
 def carried_in(value, axis, combine, identity):
@@ -66,7 +83,7 @@
     mean_sq = jnp.mean(gated * gated, axis=1, keepdims=True)
     hidden = (gated * lax.rsqrt(mean_sq + 1e-05) * norm_gain[None, :]).astype(jnp.bfloat16)
     partial_terms = jnp.dot(
-        hidden, lax.all_gather(w_out, "seq", axis=1, tiled=True), preferred_element_type=jnp.float32
+        hidden, mix_surface_by_axis(w_out, "seq"), preferred_element_type=jnp.float32
     )
     mixed = lax.psum_scatter(
         partial_terms.astype(jnp.bfloat16), "head", scatter_dimension=1, tiled=True

time: 378 us -> 483 us (1.28)
  local copies, waits for them, and re-layouts: 2.7 us -> 49.5 us
  blocking collectives: 22.2 us -> 58.3 us
  starting transfers between devices: 0.08 us -> 16.2 us
  matrix products: 15.5 us -> 20.5 us
    ppermute x0 -> x7, waiting for transfers between devices: none -> 266 us  [the longest x4 266 us: mix_surface_by_axis(): then.append(ppermute(then[-1], along_axis, pieces_in))]
    all_gather x1 -> x0, waiting for transfers between devices: 215 us -> none  [body(): lax.all_gather(w_out, 'seq', axis=1, tiled=True)]
    all_gather x1, waiting for transfers between devices: 51.5 us -> 0.01 us  [carried_in(): lax.all_gather(part.astype(kind), axis)]
    unnamed x8 -> x33, local copies, waits for them, and re-layouts: 1.26 us -> 43.8 us
    all_gather x1, blocking collectives: 22.2 us -> 58.3 us  [carried_in(): lax.all_gather(part.astype(kind), axis)]
    ppermute x0 -> x7, starting transfers between devices: none -> 16.2 us  [the longest x4 9.57 us: mix_surface_by_axis(): then.append(ppermute(then[-1], along_axis, pieces_in))]
  transfers between devices with their start and end apart: 3 -> 9, of which waited for: 3 -> 4; matrix products, arithmetic and copies ran while one was open for 4% -> 8% of each run, Pallas kernels for 0% -> 0%
where the time goes in v1:
time: 483 us; the launch traced here: 482 us
  waiting for transfers between devices  311 us (64%)
  blocking collectives  58.3 us (12%)
  local copies, waits for them, and re-layouts  49.5 us (10%)
  matrix products  20.5 us (4%)
  starting transfers between devices  16.2 us (3%)
  between operations  13.5 us (3%)
  other arithmetic  13.1 us (3%)
    ppermute x4, waiting for transfers between devices, mix_surface_by_axis(): then.append(ppermute(then[-1], along_axis, pieces_in))  266 us
    all_gather x1, blocking collectives, carried_in(): lax.all_gather(part.astype(kind), axis)  58.3 us
    reduce_scatter x1, waiting for transfers between devices, body(): lax.psum_scatter(partial_terms.astype(jnp.bfloat16), 'head', scatter_dime...  44.5 us
    unnamed x33, local copies, waits for them, and re-layouts  43.8 us
    dot_general x1, matrix products, body(): jnp.dot(hidden, mix_surface_by_axis(w_out, 'seq'), preferred_element_type...  12.2 us
    select_n x8, other arithmetic, hop(): return jax.tree.map(lambda a, b: jnp.where(reached, a, b), new, before)  10.4 us
  transfers between devices with their start and end apart: 9, of which 4 were waited for; matrix products, arithmetic and copies ran while one was open for 8% of the time, Pallas kernels for 0%

profile of v1, /device:TPU:0, one launch (start us, length us, event | category | flops | bytes accessed | tf_op | source)
XLA Modules:
  0.0 482.2 jit_solution(8558035107834390081)
XLA Ops:
  6.5 1.4 copy.27
  7.9 0.7 copy_bitcast_fusion.1
  8.7 0.6 reduce-window.6
  9.9 1.1 convolution_convert_fusion
  11.1 3.0 collective-permute-start
  14.1 3.1 collective-permute-start.4
  17.2 113.2 %collective-permute-done = bf16[1024,1024]{1,0:T(8,128)(2,1)S(1)} collective-permute-done((bf16[1024,1024]{1,0:T(8,128)(2,1)}, bf16[1024,1024]{1,0:T(8,128)(2,1)S(1)}, u32[]{:S(2)}, u32[]{:S(2)}) %collective-permute-start) | collective-permute-done | bytes 2097184 | tf_op jit(solution)/shard_map/ppermute | solution.py:14
  130.4 1.3 copy-done.3
  131.7 2.4 collective-permute-start.1
  134.1 3.1 collective-permute-start.5
  137.2 85.0 %collective-permute-done.1 = bf16[1024,1024]{1,0:T(8,128)(2,1)} collective-permute-done((bf16[1024,1024]{1,0:T(8,128)(2,1)S(1)}, bf16[1024,1024]{1,0:T(8,128)(2,1)}, u32[]{:S(2)}, u32[]{:S(2)}) %collective-permute-start.1) | collective-permute-done | bytes 2097184 | tf_op jit(solution)/shard_map/ppermute | solution.py:14
  222.1 2.6 collective-permute-start.2
  224.9 58.3 %all-gather.1 = bf16[8,1,16]{2,1,0:T(2,128)(2,1)S(1)} all-gather(bf16[1,1,16]{2,1,0:T(2,128)(2,1)S(1)} %bitcast.71), channel_id=1, replica_groups=mesh['seq'=8,'head'=4] {'seq'}, dimensions={0}, use_global_device_ids=true | all-gather | bytes 288 | tf_op jit(solution)/shard_map/all_gather | solution.py:27
  283.2 1.1 fusion.25
  284.3 3.4 fusion.12
  287.7 0.4 collective-permute-start.6
  288.1 1.6 collective-permute-start.3
  289.8 10.7 %while.14 = (s32[]{:T(128)}, f32[16,64,256]{2,1,0:T(8,128)S(1)}, s32[]{:T(128)}, bf16[8,16]{1,0:T(8,128)(2,1)S(1)}, bf16[8,16,64,256]{3,2,1,0:T(8,128)(2,1)}, /*index=5*/s32[]{:T(128)}, s32[]{:T(128)}) while((s32[]{:T(128)}, f32[16,64,256]{2,1,0:T(8,128)S(1)}, s32[]{:T(128)}, bf16[8,16]{1,0:T(8,128)(2,1)S(1)}, ...), condition=%wide.region_3.4_spmd.clone, body=%wide.region_2.3_spmd.clone.sunk | while | flops 1310740 | bytes 2621713 | solution.py:44
  289.8 1.3 fusion.37
  291.1 1.3 fusion.37
  292.4 1.3 fusion.37
  293.8 1.3 fusion.37
  295.1 1.3 fusion.37
  296.4 1.3 fusion.37
  297.8 1.3 fusion.37
  299.1 1.3 fusion.37
  300.4 2.6 fusion.14
  303.0 1.6 copy.29
  304.6 1.6 multiply_reduce_fusion
  306.2 68.2 %collective-permute-done.3 = bf16[1024,1024]{1,0:T(8,128)(2,1)} collective-permute-done((bf16[1024,1024]{1,0:T(8,128)(2,1)}, bf16[1024,1024]{1,0:T(8,128)(2,1)}, u32[]{:S(2)}, u32[]{:S(2)}) %collective-permute-start.3) | collective-permute-done | bytes 2097184 | tf_op jit(solution)/shard_map/ppermute | solution.py:14
  374.4 3.0 constant_dynamic-update-slice_fusion.15
  377.5 3.0 constant_dynamic-update-slice_fusion.14
  380.5 3.1 constant_dynamic-update-slice_fusion.13
  383.6 3.1 constant_dynamic-update-slice_fusion.12
  386.7 1.5 constant_dynamic-update-slice_fusion.11
  388.1 3.0 constant_dynamic-update-slice_fusion.10
  391.2 3.1 constant_dynamic-update-slice_fusion.9
  394.3 3.0 constant_dynamic-update-slice_fusion.8
  397.3 3.1 constant_dynamic-update-slice_fusion.7
  400.4 3.1 constant_dynamic-update-slice_fusion.6
  403.4 3.1 constant_dynamic-update-slice_fusion.5
  406.5 1.5 constant_dynamic-update-slice_fusion.4
  408.0 1.5 constant_dynamic-update-slice_fusion.3
  409.4 3.1 constant_dynamic-update-slice_fusion.2
  412.5 3.0 constant_dynamic-update-slice_fusion.1
  415.6 3.1 constant_dynamic-update-slice_fusion
  418.6 12.2 %fusion.3 = bf16[256,8192]{1,0:T(8,128)(2,1)} fusion(bf16[1024,16384]{1,0:T(8,128)(2,1)} %constant_dynamic-update-slice_fusion, s32[]{:T(128)S(6)} %select_n.45, f32[1024]{0:T(1024)S(1)} %copy-done.7, f32[256]{0:T(256)S(1)} %add_rsqrt_fusion, f32[256,1024]{1,0:T(8,128)S(1)} %copy.29, bf16[256,1024]{1,0:T(8,128)(2,1)S(1)} %copy-done.6), kind=kOutput, calls=%fused_computation.5 | convolution fusion | flops 4299423744 | bytes 22549508 | tf_op jit(solution)/shard_map/dot_general | solution.py:85
  430.9 44.5 %reduce-scatter.2.cloned.1.call-done = bf16[256,2048]{1,0:T(8,128)(2,1)} async-done(((bf16[256,8192]{1,0:T(8,128)(2,1)}), bf16[256,2048]{1,0:T(8,128)(2,1)}) %reduce-scatter.2.cloned.1.call-update) | async-done | bytes 1048592 | tf_op jit(solution)/shard_map/reduce_scatter | solution.py:88
  (44 shorter events, 1.0 us)
Async XLA Ops:
  6.5 3.4 copy-start
  6.5 380.1 %copy-start.2 = (bf16[1024,1024]{1,0:T(8,128)(2,1)S(1)}, bf16[1024,1024]{1,0:T(8,128)(2,1)}, u32[]{:S(2)}) copy-start(bf16[1024,1024]{1,0:T(8,128)(2,1)} %param.15) | copy-start | bytes 6291460
  6.5 283.2 %all-gather.4.cloned.1.call-start = ((), (), s32[]{:S(2)}) async-start(), calls=%async_computation.2 | async-start | bytes 4718592 | tf_op jit(solution)/shard_map/all_gather | solution.py:27
  7.9 216.8 %copy-start.5 = (bf16[256,1024]{0,1:T(8,128)(2,1)}, bf16[256,1024]{0,1:T(8,128)(2,1)S(1)}, u32[]{:S(2)}) copy-start(bf16[256,1024]{0,1:T(8,128)(2,1)S(1)} %copy.27) | copy-start | bytes 1572868
  11.1 464.3 %reduce-scatter.2.cloned.1.call-start = ((), (), s32[]{:S(2)}) async-start(), calls=%async_computation.1 | async-start | bytes 5242880 | tf_op jit(solution)/shard_map/reduce_scatter | solution.py:88
  11.1 119.3 %collective-permute-start = (bf16[1024,1024]{1,0:T(8,128)(2,1)}, bf16[1024,1024]{1,0:T(8,128)(2,1)S(1)}, u32[]{:S(2)}, u32[]{:S(2)}) collective-permute-start(bf16[1024,1024]{1,0:T(8,128)(2,1)} %param.15), channel_id=1, source_target_pairs={{0,4},{4,8},{8,12},{12,16},{16,20},{20,24},{24,28},{28,0},{1,5},{5... | collective-permute-start | bytes 6291464 | tf_op jit(solution)/shard_map/ppermute | solution.py:14
  14.1 120.0 %collective-permute-start.4 = (bf16[1024,1024]{1,0:T(8,128)(2,1)}, bf16[1024,1024]{1,0:T(8,128)(2,1)}, u32[]{:S(2)}, u32[]{:S(2)}) collective-permute-start(bf16[1024,1024]{1,0:T(8,128)(2,1)} %param.15), channel_id=1, source_target_pairs={{0,28},{4,0},{8,4},{12,8},{16,12},{20,16},{24,20},{28,24},{1,29},{... | collective-permute-start | bytes 6291464 | tf_op jit(solution)/shard_map/ppermute | solution.py:16
  130.4 1.3 copy-start.3
  131.7 90.4 %collective-permute-start.1 = (bf16[1024,1024]{1,0:T(8,128)(2,1)S(1)}, bf16[1024,1024]{1,0:T(8,128)(2,1)}, u32[]{:S(2)}, u32[]{:S(2)}) collective-permute-start(bf16[1024,1024]{1,0:T(8,128)(2,1)S(1)} %collective-permute-done), channel_id=1, source_target_pairs={{0,4},{4,8},{8,12},{12,16},{16,20},{20,24},{24,28},{28,0},{1,5},{5... | collective-permute-start | bytes 6291464 | tf_op jit(solution)/shard_map/ppermute | solution.py:14
  134.1 153.6 %collective-permute-start.5 = (bf16[1024,1024]{1,0:T(8,128)(2,1)}, bf16[1024,1024]{1,0:T(8,128)(2,1)}, u32[]{:S(2)}, u32[]{:S(2)}) collective-permute-start(bf16[1024,1024]{1,0:T(8,128)(2,1)} %collective-permute-done.4), channel_id=1, source_target_pairs={{0,28},{4,0},{8,4},{12,8},{16,12},{20,16},{24,20},{28,24},{1,29},{... | collective-permute-start | bytes 6291464 | tf_op jit(solution)/shard_map/ppermute | solution.py:16
  222.1 66.0 %collective-permute-start.2 = (bf16[1024,1024]{1,0:T(8,128)(2,1)}, bf16[1024,1024]{1,0:T(8,128)(2,1)}, u32[]{:S(2)}, u32[]{:S(2)}) collective-permute-start(bf16[1024,1024]{1,0:T(8,128)(2,1)} %collective-permute-done.1), channel_id=1, source_target_pairs={{0,4},{4,8},{8,12},{12,16},{16,20},{20,24},{24,28},{28,0},{1,5},{5... | collective-permute-start | bytes 6291464 | tf_op jit(solution)/shard_map/ppermute | solution.py:14
  287.7 106.5 %collective-permute-start.6 = (bf16[1024,1024]{1,0:T(8,128)(2,1)}, bf16[1024,1024]{1,0:T(8,128)(2,1)}, u32[]{:S(2)}, u32[]{:S(2)}) collective-permute-start(bf16[1024,1024]{1,0:T(8,128)(2,1)} %collective-permute-done.5), channel_id=1, source_target_pairs={{0,28},{4,0},{8,4},{12,8},{16,12},{20,16},{24,20},{28,24},{1,29},{... | collective-permute-start | bytes 6291464 | tf_op jit(solution)/shard_map/ppermute | solution.py:16
  288.1 86.3 %collective-permute-start.3 = (bf16[1024,1024]{1,0:T(8,128)(2,1)}, bf16[1024,1024]{1,0:T(8,128)(2,1)}, u32[]{:S(2)}, u32[]{:S(2)}) collective-permute-start(bf16[1024,1024]{1,0:T(8,128)(2,1)} %collective-permute-done.2), channel_id=1, source_target_pairs={{0,4},{4,8},{8,12},{12,16},{16,20},{20,24},{24,28},{28,0},{1,5},{5... | collective-permute-start | bytes 6291464 | tf_op jit(solution)/shard_map/ppermute | solution.py:14
  304.6 101.9 %copy-start.4 = (bf16[1024,1024]{1,0:T(8,128)(2,1)S(1)}, bf16[1024,1024]{1,0:T(8,128)(2,1)}, u32[]{:S(2)}) copy-start(bf16[1024,1024]{1,0:T(8,128)(2,1)} %copy-done.3) | copy-start | bytes 6291460
  306.2 112.4 %copy-start.6 = (bf16[256,1024]{1,0:T(8,128)(2,1)S(1)}, bf16[256,1024]{1,0:T(8,128)(2,1)}, u32[]{:S(2)}) copy-start(bf16[256,1024]{1,0:T(8,128)(2,1)} %param.10) | copy-start | bytes 1572868
  306.2 112.4 %copy-start.7 = (f32[1024]{0:T(1024)S(1)}, f32[1024]{0:T(1024)}, u32[]{:S(2)}) copy-start(f32[1024]{0:T(1024)} %param.14) | copy-start | bytes 12292
  406.5 68.8 %copy-start.1 = (bf16[256,1,256]{2,0,1:T(8,128)(2,1)S(1)}, bf16[256,1,256]{2,0,1:T(8,128)(2,1)}, u32[]{:S(2)}) copy-start(bf16[256,1,256]{2,0,1:T(8,128)(2,1)} %param.11) | copy-start | bytes 393220
Sparse Core Ops, SparseCore 0:
  11.2 185.8 all-gather.3
  431.0 44.2 reduce-scatter.1
